TPU v7x, 32 devices: a whole 2x2x4 slice. The times are simulated.
32 devices in a mesh: pipe: 4 (over z), ctx: 8 (over y, x, core).
Axes of the slice: x: 2, y: 2, z: 4, core: 2. Of those that a mesh axis runs over, the one named last changes fastest.
Arguments:
- queries: bfloat16 [4, 2048, 4096], P('pipe', 'ctx'), may hold values from -110 to 110
- keys: bfloat16 [4, 2048, 512], P('pipe', 'ctx'), may hold values from -4 to 4
- values: bfloat16 [4, 2048, 512], P('pipe', 'ctx'), may hold values from -6 to 6
- doc_ids: int32 [4, 8], P('pipe'), may hold values from 0 to 1, never falling along the last dimension, each value on 1 to 5 neighbouring positions
Outputs:
- handed: bfloat16 [4, 2048, 4096], P('pipe', 'ctx')
Inputs may be any that keep to these rules, and one draw needn't show every extreme that they name: doc_ids never falls along a section's blocks; each document spans 1 to 5 blocks.
All inputs are finite; a program needn't handle non-finite values.
Results may differ from a plain program's by a relative error of at most 0.004.
Values may be sent and summed in bfloat16 or wider, within the bound.
A program may use at most 320 MiB of HBM per device.

v0:
```python
import math

import jax
import jax.numpy as jnp
from jax import lax
from jax.sharding import PartitionSpec as P

HQ = 32
HK = 4
DH = 128


def shifted(value, axis, steps):
    count = lax.axis_size(axis)
    pairs = [(source, (source + steps) % count) for source in range(count)]
    return lax.ppermute(value, axis, pairs)


def shards(queries, keys, values, doc_ids):
    tok_rows = queries.shape[1]
    per_group = HQ // HK
    score_scale = 1.0 / math.sqrt(DH)
    block_index = lax.axis_index("ctx")
    first_row = block_index * tok_rows
    doc_row = doc_ids[0]
    block_ids = jnp.arange(doc_row.shape[0], dtype=jnp.int32)
    own_doc = jnp.sum(jnp.where(block_ids == block_index, doc_row, 0))
    query_pos = first_row + jnp.arange(tok_rows, dtype=jnp.int32)
    query_heads = queries[0].reshape(tok_rows, HK, per_group, DH)
    key_piece = lax.all_gather(keys[0], "ctx", axis=0, tiled=True)
    value_piece = lax.all_gather(values[0], "ctx", axis=0, tiled=True)
    key_count = key_piece.shape[0]
    key_pos = jnp.arange(key_count, dtype=jnp.int32)
    key_block = jnp.floor_divide(key_pos, tok_rows)
    key_doc = jnp.sum(
        jnp.where(key_block[:, None] == block_ids[None, :], doc_row[None, :], 0), axis=1
    )
    visible = (
        (key_doc == own_doc)[None, :]
        & (key_pos[None, :] <= query_pos[:, None])
        & (key_block >= 0)[None, :]
    )
    top_now = jnp.full((HK, per_group, tok_rows), -1e30, jnp.float32)
    key_heads = key_piece.reshape(key_count, HK, DH)
    scores = (
        jnp.einsum("qhgd,khd->hgqk", query_heads, key_heads, preferred_element_type=jnp.float32)
        * score_scale
    )
    masked = jnp.where(visible, scores, -1e30)
    top_next = jnp.maximum(top_now, jnp.max(masked, axis=-1))
    weights = jnp.where(visible, jnp.exp(masked - top_next[..., None]), 0.0)
    total_next = jnp.sum(weights, axis=-1)
    value_heads = value_piece.reshape(key_count, HK, DH)
    products = jnp.einsum(
        "hgqk,khd->hgqd",
        weights.astype(jnp.bfloat16),
        value_heads,
        preferred_element_type=jnp.float32,
    )
    finished = (top_next, total_next, products)
    top_final, total_final, acc_final = finished
    attended = (
        (acc_final / total_final[..., None])
        .transpose(2, 0, 1, 3)
        .reshape(tok_rows, HQ * DH)
        .astype(jnp.bfloat16)
    )
    return shifted(attended[None], "pipe", 1)


def solution(mesh):
    placed = (
        P("pipe", "ctx", None),
        P("pipe", "ctx", None),
        P("pipe", "ctx", None),
        P("pipe", None),
    )
    return jax.shard_map(
        shards, mesh=mesh, in_specs=placed, out_specs=P("pipe", "ctx", None), check_vma=False
    )
```

profile of v0, /device:TPU:0, one launch (start us, length us, event | category | flops | bytes accessed | tf_op | source)
XLA Modules:
  0.0 178.7 jit_solution(3291278952781805247)
XLA Ops:
  6.5 0.0 all-gather.5.cloned.1.call-start
  6.5 1.8 %copy.15 = bf16[1,256,512]{1,2,0:T(8,128)(2,1)} copy(bf16[1,256,512]{2,1,0:T(8,128)(2,1)} %param.5) | data formatting | bytes 524288 | tf_op args[1]
  8.3 0.0 all-gather.5.cloned.1.call-update
  8.4 0.0 all-gather.7.cloned.1.call-start
  8.4 0.7 all-gather.7.cloned.1.call-update
  9.1 1.4 fusion.16
  10.5 2.1 %copy.26 = bf16[32,8,32,128]{3,2,1,0:T(8,128)(2,1)S(1)} copy(bf16[32,8,32,128]{3,1,2,0:T(8,128)(2,1)} %bitcast.39) | data formatting | bytes 4194304
  12.6 0.7 select_reduce_fusion
  13.3 0.7 broadcast_compare_fusion
  14.0 1.4 fusion.12
  15.5 24.7 %all-gather.5.cloned.1.call-done = bf16[1,2048,512]{1,2,0:T(8,128)(2,1)} async-done(((bf16[1,256,512]{1,2,0:T(8,128)(2,1)}), bf16[1,2048,512]{1,2,0:T(8,128)(2,1)}) %all-gather.5.cloned.1.call-update) | async-done | bytes 2097168 | tf_op jit(solution)/shard_map/all_gather | solution.py:30
  40.2 26.2 %fusion = (f32[4,8,256]{2,1,0:T(8,128)S(1)}, f32[4,2048,256,8]{2,1,3,0:T(8,128)}) fusion(pred[256,2048]{0,1:T(8,128)(4,1)S(1)} %fusion.12, bf16[2048,4,128,1]{0,2,3,1:T(8,128)(2,1)} %bitcast.38, bf16[256,4,8,128]{3,2,1,0:T(8,128)(2,1)S(1)} %bitcast.37), kind=kOutput, calls=%fused_computation.2 | convolution fusion | flops 4345290752 | bytes 71860224 | tf_op jit(solution)/shard_map/qhgd,khd->hgqk/dot_general | solution.py:46
  66.4 21.8 %fusion.1 = f32[4,8,256]{2,1,0:T(8,128)S(1)} fusion(f32[4,2048,256,8]{2,1,3,0:T(8,128)} %get-tuple-element.6, f32[4,8,256]{2,1,0:T(8,128)S(1)} %broadcast_maximum_fusion, pred[256,2048]{0,1:T(8,128)(4,1)S(1)} %fusion.12), kind=kLoop, calls=%fused_computation.3 | loop fusion | flops 83877888 | bytes 67698688 | tf_op jit(solution)/shard_map/reduce_sum | solution.py:52
  88.2 0.0 all-gather.7.cloned.1.call-done
  88.3 2.9 %copy.18 = bf16[1,2048,512]{1,2,0:T(8,128)(2,1)S(1)} copy(bf16[1,2048,512]{2,1,0:T(8,128)(2,1)} %all-gather.7.cloned.1.call-done) | data formatting | bytes 4194304 | tf_op jit(solution)/shard_map/all_gather | solution.py:31
  91.2 26.8 %fusion.6 = bf16[256,4,8,128]{0,3,2,1:T(8,128)(2,1)} fusion(bf16[2048,4,128,1]{0,2,3,1:T(8,128)(2,1)S(1)} %bitcast.40, f32[4,2048,256,8]{2,1,3,0:T(8,128)} %get-tuple-element.6, f32[4,8,256]{2,1,0:T(8,128)S(1)} %broadcast_maximum_fusion, pred[256,2048]{0,1:T(8,128)(4,1)S(1)} %fusion.12, f32[256,4,8]{0,2,1:T(8,128)S(1)} %bitcast.42), kind=kOutput, calls=%fused_computation.8 | convolution fusion | flops 4380950528 | bytes 71892992 | tf_op jit(solution)/shard_map/hgqk,khd->hgqd/dot_general | solution.py:54
  118.0 2.9 %copy.20 = bf16[1,256,4096]{2,1,0:T(8,128)(2,1)S(1)} copy(bf16[1,256,4096]{1,2,0:T(8,128)(2,1)} %bitcast.41) | data formatting | bytes 4194304 | tf_op jit(solution)/shard_map/convert_element_type | solution.py:66
  120.9 1.5 collective-permute-start
  122.4 48.1 %collective-permute-done = bf16[1,256,4096]{2,1,0:T(8,128)(2,1)S(1)} collective-permute-done((bf16[1,256,4096]{2,1,0:T(8,128)(2,1)S(1)}, bf16[1,256,4096]{2,1,0:T(8,128)(2,1)S(1)}, u32[]{:S(2)}, u32[]{:S(2)}) %collective-permute-start) | collective-permute-done | bytes 2097184 | tf_op jit(solution)/shard_map/ppermute | solution.py:16
  170.6 1.3 copy.32
  (3 shorter events, 0.0 us)
Async XLA Ops:
  6.5 33.6 %all-gather.5.cloned.1.call-start = ((), (), s32[]{:S(2)}) async-start(), calls=%async_computation | async-start | bytes 2359296 | tf_op jit(solution)/shard_map/all_gather | solution.py:30
  8.4 79.9 %all-gather.7.cloned.1.call-start = ((), (), s32[]{:S(2)}) async-start(), calls=%async_computation.1 | async-start | bytes 2359296 | tf_op jit(solution)/shard_map/all_gather | solution.py:31
  120.9 49.7 %collective-permute-start = (bf16[1,256,4096]{2,1,0:T(8,128)(2,1)S(1)}, bf16[1,256,4096]{2,1,0:T(8,128)(2,1)S(1)}, u32[]{:S(2)}, u32[]{:S(2)}) collective-permute-start(bf16[1,256,4096]{2,1,0:T(8,128)(2,1)S(1)} %copy.20), channel_id=1, source_target_pairs={{0,8},{8,16},{16,24},{24,0},{1,9},{9,17},{17,25},{25,1},{2,10},{10... | collective-permute-start | bytes 6291464 | tf_op jit(solution)/shard_map/ppermute | solution.py:16
Sparse Core Ops, SparseCore 0:
  9.2 30.8 all-gather.4
  42.0 27.8 all-gather.6
where the time goes:
time: 179 us
  waiting for transfers between devices  73.6 us (41%)
  matrix products  53 us (30%)
  other arithmetic  26.1 us (15%)
  between operations  13.5 us (8%)
  local copies, waits for them, and re-layouts  11 us (6%)
    ppermute x1, waiting for transfers between devices, shifted(): return lax.ppermute(value, axis, pairs)  48.1 us
    dot_general x1, matrix products, shards(): jnp.einsum('hgqk,khd->hgqd', weights.astype(jnp.bfloat16), value_heads, p...  26.8 us
    dot_general x1, matrix products, shards(): jnp.einsum('qhgd,khd->hgqk', query_heads, key_heads, preferred_element_ty...  26.2 us
    all_gather x1, waiting for transfers between devices, shards(): key_piece = lax.all_gather(keys[0], 'ctx', axis=0, tiled=True)  24.7 us
    reduce_sum x1, other arithmetic, shards(): total_next = jnp.sum(weights, axis=-1)  21.8 us
    unnamed x3, local copies, waits for them, and re-layouts  5.17 us
  transfers between devices with their start and end apart: 3, of which 2 were waited for; matrix products, arithmetic and copies ran while one was open for 30% of the time, Pallas kernels for 0%

commit v1 on v0

v1 whole, which is shorter than its diff:
```python
import functools
import math

import jax
import jax.numpy as jnp
from jax import lax
from jax.experimental import pallas as pl
from jax.experimental.pallas import tpu as pltpu
from jax.sharding import PartitionSpec as P

HQ = 32
HK = 4
DH = 128
PER_GROUP = HQ // HK
STEP_HEADS = 2
HIDDEN = 1e30
MESH = pl.DeviceIdType.MESH


def kernel(
    n_pipe,
    n_ctx,
    window,
    rows,
    doc_ref,
    q_ref,
    k_ref,
    v_ref,
    out_ref,
    qbuf,
    kbuf,
    vbuf,
    obuf,
    bias,
    q_sem,
    own_sem,
    kv_send,
    kv_recv,
    z_send,
    z_recv,
    o_send,
    o_recv,
):
    pipe = lax.axis_index("pipe")
    ctx = lax.axis_index("ctx")
    right = lax.rem(pipe + 1, n_pipe)
    left = lax.rem(pipe + n_pipe - 1, n_pipe)
    moved = HK - 1
    group_cols = PER_GROUP * DH
    step_cols = STEP_HEADS * DH
    steps = HQ // STEP_HEADS
    group_steps = PER_GROUP // STEP_HEADS
    sent_steps = moved * group_steps
    last = window - 1

    barrier = pltpu.get_barrier_semaphore()
    pl.semaphore_signal(barrier, inc=1, device_id=(left, ctx), device_id_type=MESH)
    pl.semaphore_signal(barrier, inc=1, device_id=(right, ctx), device_id_type=MESH)
    for d in range(1, window):

        @pl.when(ctx >= d)
        def _():
            pl.semaphore_signal(barrier, inc=1, device_id=(pipe, ctx - d), device_id_type=MESH)

        @pl.when(ctx + d < n_ctx)
        def _():
            pl.semaphore_signal(barrier, inc=1, device_id=(pipe, ctx + d), device_id_type=MESH)

    def own_copies(g):
        cols = pl.ds(pl.multiple_of(g * DH, DH), DH)
        place = pl.ds(last * rows, rows)
        return (
            pltpu.make_async_copy(k_ref.at[:, cols], kbuf.at[g, place], own_sem.at[0, g]),
            pltpu.make_async_copy(v_ref.at[:, cols], vbuf.at[g, place], own_sem.at[1, g]),
        )

    def q_copy(g):
        cols = pl.ds(pl.multiple_of(g * group_cols, group_cols), group_cols)
        return pltpu.make_async_copy(q_ref.at[:, cols], qbuf.at[:, cols], q_sem.at[g])

    def gather_copies(g, d):
        source = pl.ds(last * rows, rows)
        place = pl.ds((last - d) * rows, rows)
        return [
            pltpu.make_async_remote_copy(
                src_ref=buf.at[g, source],
                dst_ref=buf.at[g, place],
                send_sem=kv_send.at[which, g, d - 1],
                recv_sem=kv_recv.at[which, g, d - 1],
                device_id=(pipe, lax.rem(ctx + d, n_ctx)),
                device_id_type=MESH,
            )
            for which, buf in ((0, kbuf), (1, vbuf))
        ]

    def to_right(source, target, at):
        return pltpu.make_async_remote_copy(
            src_ref=source,
            dst_ref=target,
            send_sem=z_send.at[at],
            recv_sem=z_recv.at[at],
            device_id=(right, ctx),
            device_id_type=MESH,
        )

    def moved_copies():
        cols = pl.ds(moved * DH, DH)
        q_cols = pl.ds(moved * group_cols, group_cols)
        place = pl.ds(last * rows, rows)
        return (
            to_right(k_ref.at[:, cols], kbuf.at[moved, place], 0),
            to_right(v_ref.at[:, cols], vbuf.at[moved, place], 1),
            to_right(bias.at[0], bias.at[1], 2),
            to_right(q_ref.at[:, q_cols], qbuf.at[:, q_cols], 3),
        )

    def out_copy(step):
        cols = pl.ds(pl.multiple_of(step * step_cols, step_cols), step_cols)
        return pltpu.make_async_remote_copy(
            src_ref=obuf.at[:, cols],
            dst_ref=out_ref.at[:, cols],
            send_sem=o_send.at[step],
            recv_sem=o_recv.at[step],
            device_id=(right, ctx),
            device_id_type=MESH,
        )

    def out_local(step):
        cols = pl.ds(pl.multiple_of(step * step_cols, step_cols), step_cols)
        return pltpu.make_async_copy(obuf.at[:, cols], out_ref.at[:, cols], o_send.at[step])

    for g in range(moved):
        for copy in own_copies(g):
            copy.start()
        q_copy(g).start()

    bias[0] = jnp.zeros(bias.shape[1:], jnp.float32)
    own_doc = doc_ref[0, ctx]
    for d in range(window):
        block = jnp.maximum(ctx - d, 0)
        seen = (doc_ref[0, block] == own_doc) & (ctx >= d)
        bias[0, d : d + 1, :] = jnp.full((1, DH), jnp.where(seen, 0.0, HIDDEN), jnp.float32)

    for d in range(1, window):

        @pl.when(ctx < d)
        def _():
            place = pl.ds((last - d) * rows, rows)
            for g in range(HK):
                kbuf[g, place, :] = jnp.zeros((rows, DH), kbuf.dtype)
                vbuf[g, place, :] = jnp.zeros((rows, DH), vbuf.dtype)

    met = 2
    for d in range(1, window):
        met = met + jnp.where(ctx >= d, 1, 0) + jnp.where(ctx + d < n_ctx, 1, 0)
    pl.semaphore_wait(barrier, met)

    for copy in moved_copies():
        copy.start()

    def start_gather(g):
        @pl.when(g < moved)
        def _():
            for copy in own_copies(g):
                copy.wait()

        @pl.when(g == moved)
        def _():
            for copy in moved_copies()[:3]:
                copy.wait_recv()

        for d in range(1, window):

            @pl.when(ctx + d < n_ctx)
            def _():
                for copy in gather_copies(g, d):
                    copy.start()

    def end_gather(g):
        for d in range(1, window):

            @pl.when(ctx >= d)
            def _():
                for copy in gather_copies(g, d):
                    copy.wait_recv()

    start_gather(0)
    factor = math.log2(math.e) / math.sqrt(DH)

    @pl.loop(0, steps)
    def _(step):
        g = step // group_steps

        @pl.when(lax.rem(step, group_steps) == 0)
        def _():
            @pl.when(g < moved)
            def _():
                q_copy(g).wait()

            @pl.when(g == moved)
            def _():
                moved_copies()[3].wait_recv()

            end_gather(g)

            @pl.when(g < moved)
            def _():
                start_gather(g + 1)

        which = jnp.where(g == moved, 1, 0)
        causal = lax.broadcasted_iota(jnp.int32, (rows, rows), 0) >= lax.broadcasted_iota(
            jnp.int32, (rows, rows), 1
        )
        for at in range(STEP_HEADS):
            cols = pl.ds(pl.multiple_of(step * step_cols + at * DH, DH), DH)
            query = qbuf[:, cols]
            scores = []
            top = None
            for d in range(window):
                place = pl.ds((last - d) * rows, rows)
                part = lax.dot_general(
                    query,
                    kbuf[g, place, :],
                    (((1,), (1,)), ((), ())),
                    preferred_element_type=jnp.float32,
                )
                if d == 0:
                    part = jnp.where(causal, part, -HIDDEN)
                scores.append(part)
                lanes = part[:, :DH]
                for c in range(1, rows // DH):
                    lanes = jnp.maximum(lanes, part[:, c * DH : (c + 1) * DH])
                if d > 0:
                    lanes = lanes - bias[which, d : d + 1, :]
                top = lanes if top is None else jnp.maximum(top, lanes)
            row_top = jnp.max(top, axis=1, keepdims=True)
            total = None
            acc = None
            for d in range(window):
                place = pl.ds((last - d) * rows, rows)
                offset = row_top
                if d > 0:
                    offset = row_top + bias[which, d : d + 1, :1]
                weights = jnp.exp2((scores[d] - offset) * factor)
                for c in range(rows // DH):
                    lanes = weights[:, c * DH : (c + 1) * DH]
                    total = lanes if total is None else total + lanes
                product = jnp.dot(
                    weights.astype(jnp.bfloat16),
                    vbuf[g, place, :],
                    preferred_element_type=jnp.float32,
                )
                acc = product if acc is None else acc + product
            row_total = jnp.sum(total, axis=1, keepdims=True)
            obuf[:, cols] = (acc / row_total).astype(obuf.dtype)

        @pl.when(g < moved)
        def _():
            out_copy(step).start()

        @pl.when(g == moved)
        def _():
            out_local(step).start()

    for copy in moved_copies():
        copy.wait_send()

    @pl.loop(0, HK)
    def _(g):
        for d in range(1, window):

            @pl.when(ctx + d < n_ctx)
            def _():
                for copy in gather_copies(g, d):
                    copy.wait_send()

    @pl.loop(sent_steps, steps)
    def _(step):
        out_local(step).wait()

    @pl.loop(0, sent_steps)
    def _(step):
        out_copy(step).wait_send()
        out_copy(step).wait_recv()


def shards(n_pipe, n_ctx, queries, keys, values, doc_ids):
    rows = queries.shape[1]
    window = n_ctx // 2 + 1
    steps = HQ // STEP_HEADS
    bias_rows = (window + 7) // 8 * 8
    dma = pltpu.SemaphoreType.DMA
    anywhere = pl.BlockSpec(memory_space=pl.ANY)
    handed = pl.pallas_call(
        functools.partial(kernel, n_pipe, n_ctx, window, rows),
        out_shape=jax.ShapeDtypeStruct((rows, HQ * DH), jnp.bfloat16),
        in_specs=[pl.BlockSpec(memory_space=pltpu.SMEM), anywhere, anywhere, anywhere],
        out_specs=anywhere,
        scratch_shapes=[
            pltpu.VMEM((rows, HQ * DH), jnp.bfloat16),
            pltpu.VMEM((HK, window * rows, DH), jnp.bfloat16),
            pltpu.VMEM((HK, window * rows, DH), jnp.bfloat16),
            pltpu.VMEM((rows, HQ * DH), jnp.bfloat16),
            pltpu.VMEM((2, bias_rows, DH), jnp.float32),
            dma((HK,)),
            dma((2, HK)),
            dma((2, HK, window - 1)),
            dma((2, HK, window - 1)),
            dma((4,)),
            dma((4,)),
            dma((steps,)),
            dma((steps,)),
        ],
        compiler_params=pltpu.CompilerParams(
            collective_id=0, has_side_effects=True, vmem_limit_bytes=48 * 1024 * 1024
        ),
        name="relay_attention",
    )(doc_ids, queries[0], keys[0], values[0])
    return handed[None]


def solution(mesh):
    placed = (
        P("pipe", "ctx", None),
        P("pipe", "ctx", None),
        P("pipe", "ctx", None),
        P("pipe", None),
    )
    return jax.shard_map(
        functools.partial(shards, mesh.shape["pipe"], mesh.shape["ctx"]),
        mesh=mesh,
        in_specs=placed,
        out_specs=P("pipe", "ctx", None),
        check_vma=False,
    )
```

time: 179 us -> 76.5 us (0.43)
  the two profiles are of different devices: /device:TPU:0 before, /device:TPU:5 now
where the time goes in v1:
time: 76.5 us; the launch traced here: 76.3 us
  Pallas kernels  70.8 us (93%)
  local copies, waits for them, and re-layouts  5.47 us (7%)
    pallas_call x1, Pallas kernels, shards(): pl.pallas_call(functools.partial(kernel, n_pipe, n_ctx, window, rows), ou...  70.8 us
    unnamed x9, local copies, waits for them, and re-layouts  5.47 us

profile of v1, /device:TPU:5, one launch (start us, length us, event | category | flops | bytes accessed | tf_op | source)
XLA Modules:
  0.0 76.3 jit_solution(17727612495863400252)
XLA Ops:
  0.0 0.0 copy-start
  0.0 1.6 %copy-done = bf16[1,256,4096]{2,1,0:T(8,128)(2,1)S(1)} copy-done((bf16[1,256,4096]{2,1,0:T(8,128)(2,1)S(1)}, bf16[1,256,4096]{2,1,0:T(8,128)(2,1)}, u32[]{:S(2)}) %copy-start) | copy-done | bytes 2097176
  1.6 0.0 copy-start.1
  1.6 0.9 %copy-done.1 = bf16[1,256,512]{2,1,0:T(8,128)(2,1)S(1)} copy-done((bf16[1,256,512]{2,1,0:T(8,128)(2,1)S(1)}, bf16[1,256,512]{2,1,0:T(8,128)(2,1)}, u32[]{:S(2)}) %copy-start.1) | copy-done | bytes 262168
  2.5 0.0 copy-start.2
  2.5 0.9 %copy-done.2 = bf16[1,256,512]{2,1,0:T(8,128)(2,1)S(1)} copy-done((bf16[1,256,512]{2,1,0:T(8,128)(2,1)S(1)}, bf16[1,256,512]{2,1,0:T(8,128)(2,1)}, u32[]{:S(2)}) %copy-start.2) | copy-done | bytes 262168
  3.5 0.0 copy-start.3
  3.5 0.7 copy-done.3
  4.1 70.8 %relay_attention.1 = bf16[256,4096]{1,0:T(8,128)(2,1)S(1)} custom-call(s32[1,8]{1,0:T(1,128)S(1)} %copy-done.3, bf16[256,4096]{1,0:T(8,128)(2,1)S(1)} %bitcast.5, bf16[256,512]{1,0:T(8,128)(2,1)S(1)} %bitcast.6, bf16[256,512]{1,0:T(8,128)(2,1)S(1)} %bitcast.7), custom_call_target="tpu_custom_call" | custom-call | tf_op jit(solution)/shard_map/relay_attention/pallas_call | solution.py:294
  75.0 1.3 %copy.6 = bf16[1,256,4096]{2,1,0:T(8,128)(2,1)} copy(bf16[1,256,4096]{2,1,0:T(8,128)(2,1)S(1)} %bitcast.4) | data formatting | bytes 4194304
Async XLA Ops:
  0.0 1.6 %copy-start = (bf16[1,256,4096]{2,1,0:T(8,128)(2,1)S(1)}, bf16[1,256,4096]{2,1,0:T(8,128)(2,1)}, u32[]{:S(2)}) copy-start(bf16[1,256,4096]{2,1,0:T(8,128)(2,1)} %param.4) | copy-start | bytes 6291460
  1.6 0.9 %copy-start.1 = (bf16[1,256,512]{2,1,0:T(8,128)(2,1)S(1)}, bf16[1,256,512]{2,1,0:T(8,128)(2,1)}, u32[]{:S(2)}) copy-start(bf16[1,256,512]{2,1,0:T(8,128)(2,1)} %param.5) | copy-start | bytes 786436
  2.5 0.9 %copy-start.2 = (bf16[1,256,512]{2,1,0:T(8,128)(2,1)S(1)}, bf16[1,256,512]{2,1,0:T(8,128)(2,1)}, u32[]{:S(2)}) copy-start(bf16[1,256,512]{2,1,0:T(8,128)(2,1)} %param.6) | copy-start | bytes 786436
  3.5 0.7 copy-start.3

commit v2 on v1

--- a/solution.py
+++ b/solution.py
@@ -22,7 +22,7 @@
     n_ctx,
     window,
     rows,
-    doc_ref,
+    doc_hbm,
     q_ref,
     k_ref,
     v_ref,
@@ -32,6 +32,8 @@
     vbuf,
     obuf,
     bias,
+    doc_ref,
+    doc_sem,
     q_sem,
     own_sem,
     kv_send,
@@ -56,7 +58,9 @@
     barrier = pltpu.get_barrier_semaphore()
     pl.semaphore_signal(barrier, inc=1, device_id=(left, ctx), device_id_type=MESH)
     pl.semaphore_signal(barrier, inc=1, device_id=(right, ctx), device_id_type=MESH)
-    for d in range(1, window):
+    sibling_core = ctx + 1 - 2 * lax.rem(ctx, 2)
+    pl.semaphore_signal(barrier, inc=1, device_id=(pipe, sibling_core), device_id_type=MESH)
+    for d in range(2, window, 2):
 
         @pl.when(ctx >= d)
         def _():
@@ -78,20 +82,56 @@
         cols = pl.ds(pl.multiple_of(g * group_cols, group_cols), group_cols)
         return pltpu.make_async_copy(q_ref.at[:, cols], qbuf.at[:, cols], q_sem.at[g])
 
-    def gather_copies(g, d):
-        source = pl.ds(last * rows, rows)
-        place = pl.ds((last - d) * rows, rows)
+    def kv_copies(g, source, target, ctx_to):
+        from_rows = pl.ds(pl.multiple_of((last - source) * rows, rows), rows)
+        to_rows = pl.ds(pl.multiple_of((last - target) * rows, rows), rows)
         return [
             pltpu.make_async_remote_copy(
-                src_ref=buf.at[g, source],
-                dst_ref=buf.at[g, place],
-                send_sem=kv_send.at[which, g, d - 1],
-                recv_sem=kv_recv.at[which, g, d - 1],
-                device_id=(pipe, lax.rem(ctx + d, n_ctx)),
+                src_ref=buf.at[g, from_rows],
+                dst_ref=buf.at[g, to_rows],
+                send_sem=kv_send.at[which, g, target - 1],
+                recv_sem=kv_recv.at[which, g, target - 1],
+                device_id=(pipe, ctx_to),
                 device_id_type=MESH,
             )
             for which, buf in ((0, kbuf), (1, vbuf))
         ]
+
+    def direct(g, d):
+        return kv_copies(g, 0, d, lax.rem(ctx + d, n_ctx))
+
+    core = lax.rem(ctx, 2)
+    turn = 1 - 2 * core
+    sibling = ctx + turn
+
+    def relay(g, d):
+        return kv_copies(g, d, d + turn, sibling)
+
+    def for_direct(do):
+        for d in range(2, window, 2):
+            pl.when(ctx + d < n_ctx)(functools.partial(do, d))
+
+    def for_relay(do):
+        for d in range(0, window, 2):
+            if d == 0:
+                fits = core == 0
+            elif d == last:
+                fits = (core == 1) & (ctx >= d)
+            else:
+                fits = ctx >= d
+            pl.when(fits)(functools.partial(do, d))
+
+    def start_all(make, g, d):
+        for copy in make(g, d):
+            copy.start()
+
+    def end_send(make, g, d):
+        for copy in make(g, d):
+            copy.wait_send()
+
+    def wait_block(g, d):
+        for copy in kv_copies(g, 0, d, sibling):
+            copy.wait_recv()
 
     def to_right(source, target, at):
         return pltpu.make_async_remote_copy(
@@ -129,11 +169,14 @@
         cols = pl.ds(pl.multiple_of(step * step_cols, step_cols), step_cols)
         return pltpu.make_async_copy(obuf.at[:, cols], out_ref.at[:, cols], o_send.at[step])
 
+    doc_copy = pltpu.make_async_copy(doc_hbm, doc_ref, doc_sem)
+    doc_copy.start()
     for g in range(moved):
         for copy in own_copies(g):
             copy.start()
         q_copy(g).start()
 
+    doc_copy.wait()
     bias[0] = jnp.zeros(bias.shape[1:], jnp.float32)
     own_doc = doc_ref[0, ctx]
     for d in range(window):
@@ -150,15 +193,15 @@
                 kbuf[g, place, :] = jnp.zeros((rows, DH), kbuf.dtype)
                 vbuf[g, place, :] = jnp.zeros((rows, DH), vbuf.dtype)
 
-    met = 2
-    for d in range(1, window):
+    met = 3
+    for d in range(2, window, 2):
         met = met + jnp.where(ctx >= d, 1, 0) + jnp.where(ctx + d < n_ctx, 1, 0)
     pl.semaphore_wait(barrier, met)
 
     for copy in moved_copies():
         copy.start()
 
-    def start_gather(g):
+    def start_direct(g):
         @pl.when(g < moved)
         def _():
             for copy in own_copies(g):
@@ -169,22 +212,20 @@
             for copy in moved_copies()[:3]:
                 copy.wait_recv()
 
-        for d in range(1, window):
-
-            @pl.when(ctx + d < n_ctx)
-            def _():
-                for copy in gather_copies(g, d):
-                    copy.start()
+        for_direct(lambda d: start_all(direct, g, d))
+
+    def start_relay(g):
+        for d in range(2, window, 2):
+            pl.when(ctx >= d)(functools.partial(wait_block, g, d))
+        for_relay(lambda d: start_all(relay, g, d))
 
     def end_gather(g):
-        for d in range(1, window):
-
-            @pl.when(ctx >= d)
-            def _():
-                for copy in gather_copies(g, d):
-                    copy.wait_recv()
-
-    start_gather(0)
+        for d in range(1, window, 2):
+            pl.when(ctx >= d)(functools.partial(wait_block, g, d))
+
+    start_direct(0)
+    start_direct(1)
+    start_relay(0)
     factor = math.log2(math.e) / math.sqrt(DH)
 
     @pl.loop(0, steps)
@@ -203,9 +244,13 @@
 
             end_gather(g)
 
-            @pl.when(g < moved)
+            @pl.when(g + 1 < moved)
             def _():
-                start_gather(g + 1)
+                start_direct(g + 2)
+
+        @pl.when((lax.rem(step, group_steps) == group_steps // 2) & (g < moved))
+        def _():
+            start_relay(g + 1)
 
         which = jnp.where(g == moved, 1, 0)
         causal = lax.broadcasted_iota(jnp.int32, (rows, rows), 0) >= lax.broadcasted_iota(
@@ -267,12 +312,8 @@
 
     @pl.loop(0, HK)
     def _(g):
-        for d in range(1, window):
-
-            @pl.when(ctx + d < n_ctx)
-            def _():
-                for copy in gather_copies(g, d):
-                    copy.wait_send()
+        for_direct(lambda d: end_send(direct, g, d))
+        for_relay(lambda d: end_send(relay, g, d))
 
     @pl.loop(sent_steps, steps)
     def _(step):
@@ -294,7 +335,7 @@
     handed = pl.pallas_call(
         functools.partial(kernel, n_pipe, n_ctx, window, rows),
         out_shape=jax.ShapeDtypeStruct((rows, HQ * DH), jnp.bfloat16),
-        in_specs=[pl.BlockSpec(memory_space=pltpu.SMEM), anywhere, anywhere, anywhere],
+        in_specs=[pl.BlockSpec(memory_space=pltpu.HBM)] * 4,
         out_specs=anywhere,
         scratch_shapes=[
             pltpu.VMEM((rows, HQ * DH), jnp.bfloat16),
@@ -302,6 +343,8 @@
             pltpu.VMEM((HK, window * rows, DH), jnp.bfloat16),
             pltpu.VMEM((rows, HQ * DH), jnp.bfloat16),
             pltpu.VMEM((2, bias_rows, DH), jnp.float32),
+            pltpu.SMEM(doc_ids.shape, jnp.int32),
+            dma,
             dma((HK,)),
             dma((2, HK)),
             dma((2, HK, window - 1)),
@@ -315,7 +358,7 @@
             collective_id=0, has_side_effects=True, vmem_limit_bytes=48 * 1024 * 1024
         ),
         name="relay_attention",
-    )(doc_ids, queries[0], keys[0], values[0])
+    )(*(pltpu.with_memory_space_constraint(x, pltpu.HBM) for x in (doc_ids, queries[0], keys[0], values[0])))
     return handed[None]
 
 

time: 76.5 us -> 57.9 us (0.76)
  the two profiles are of different devices: /device:TPU:5 before, /device:TPU:0 now
where the time goes in v2:
time: 57.9 us; the launch traced here: 57.4 us
  Pallas kernels  56.1 us (97%)
  local copies, waits for them, and re-layouts  1.32 us (2%)
    pallas_call x1, Pallas kernels, shards(): pl.pallas_call(functools.partial(kernel, n_pipe, n_ctx, window, rows), ou...  56.1 us
    unnamed x1, local copies, waits for them, and re-layouts  1.32 us

profile of v2, /device:TPU:0, one launch (start us, length us, event | category | flops | bytes accessed | tf_op | source)
XLA Modules:
  0.0 57.4 jit_solution(17024966520463306863)
XLA Ops:
  0.0 56.1 %relay_attention.1 = bf16[256,4096]{1,0:T(8,128)(2,1)S(1)} custom-call(s32[1,8]{1,0:T(1,128)} %doc_hbm.1, bf16[256,4096]{1,0:T(8,128)(2,1)} %bitcast.5, bf16[256,512]{1,0:T(8,128)(2,1)} %bitcast.6, bf16[256,512]{1,0:T(8,128)(2,1)} %bitcast.7), custom_call_target="tpu_custom_call" | custom-call | tf_op jit(solution)/shard_map/relay_attention/pallas_call | solution.py:335
  56.1 1.3 %copy.6 = bf16[1,256,4096]{2,1,0:T(8,128)(2,1)} copy(bf16[1,256,4096]{2,1,0:T(8,128)(2,1)S(1)} %bitcast.4) | data formatting | bytes 4194304

commit v3 on v2

--- a/solution.py
+++ b/solution.py
@@ -107,18 +107,32 @@
     def relay(g, d):
         return kv_copies(g, d, d + turn, sibling)
 
+    odd_chip = lax.rem(ctx // 2, 2) == 1
+    even_chip = lax.rem(ctx // 2, 2) == 0
+
+    def forward(g, d):
+        return kv_copies(g, d, d - 2, lax.rem(ctx + n_ctx - 2, n_ctx))
+
     def for_direct(do):
         for d in range(2, window, 2):
-            pl.when(ctx + d < n_ctx)(functools.partial(do, d))
-
-    def for_relay(do):
+            fits = even_chip if d == 2 else ctx + d < n_ctx
+            pl.when(fits)(functools.partial(do, d))
+
+    def for_forward(do):
+        pl.when(odd_chip & (ctx >= 4))(functools.partial(do, 4))
+
+    def for_relay(do, late):
         for d in range(0, window, 2):
+            if late and d != 2:
+                continue
             if d == 0:
                 fits = core == 0
-            elif d == last:
-                fits = (core == 1) & (ctx >= d)
+            elif d == 2:
+                fits = (even_chip if late else odd_chip) & (ctx >= d)
             else:
                 fits = ctx >= d
+            if d == last:
+                fits = fits & (core == 1)
             pl.when(fits)(functools.partial(do, d))
 
     def start_all(make, g, d):
@@ -202,30 +216,35 @@
         copy.start()
 
     def start_direct(g):
-        @pl.when(g < moved)
-        def _():
+        if g < moved:
             for copy in own_copies(g):
                 copy.wait()
-
-        @pl.when(g == moved)
-        def _():
+        else:
             for copy in moved_copies()[:3]:
                 copy.wait_recv()
-
         for_direct(lambda d: start_all(direct, g, d))
 
-    def start_relay(g):
+    def pass_on(g):
         for d in range(2, window, 2):
-            pl.when(ctx >= d)(functools.partial(wait_block, g, d))
-        for_relay(lambda d: start_all(relay, g, d))
+            fits = odd_chip if d == 2 else ctx >= d
+            pl.when(fits)(functools.partial(wait_block, g, d))
+        for_forward(lambda d: start_all(forward, g, d))
+        for_relay(lambda d: start_all(relay, g, d), False)
+
+    def pass_late(g):
+        pl.when(even_chip & (ctx >= 2))(functools.partial(wait_block, g, 2))
+        for_relay(lambda d: start_all(relay, g, d), True)
 
     def end_gather(g):
         for d in range(1, window, 2):
             pl.when(ctx >= d)(functools.partial(wait_block, g, d))
 
     start_direct(0)
+    pass_on(0)
     start_direct(1)
-    start_relay(0)
+    pass_late(0)
+    pass_on(1)
+    start_direct(2)
     factor = math.log2(math.e) / math.sqrt(DH)
 
     @pl.loop(0, steps)
@@ -244,13 +263,20 @@
 
             end_gather(g)
 
-            @pl.when(g + 1 < moved)
-            def _():
-                start_direct(g + 2)
-
-        @pl.when((lax.rem(step, group_steps) == group_steps // 2) & (g < moved))
-        def _():
-            start_relay(g + 1)
+        @pl.when(step == 1)
+        def _():
+            pass_late(1)
+            pass_on(2)
+            start_direct(3)
+
+        @pl.when(step == 3)
+        def _():
+            pass_late(2)
+            pass_on(3)
+
+        @pl.when(step == 5)
+        def _():
+            pass_late(3)
 
         which = jnp.where(g == moved, 1, 0)
         causal = lax.broadcasted_iota(jnp.int32, (rows, rows), 0) >= lax.broadcasted_iota(
@@ -278,20 +304,21 @@
                 if d > 0:
                     lanes = lanes - bias[which, d : d + 1, :]
                 top = lanes if top is None else jnp.maximum(top, lanes)
-            row_top = jnp.max(top, axis=1, keepdims=True)
+            row_top = jnp.broadcast_to(jnp.max(top, axis=1, keepdims=True), (rows, DH))
             total = None
             acc = None
             for d in range(window):
                 place = pl.ds((last - d) * rows, rows)
                 offset = row_top
                 if d > 0:
-                    offset = row_top + bias[which, d : d + 1, :1]
-                weights = jnp.exp2((scores[d] - offset) * factor)
+                    offset = row_top + bias[which, d : d + 1, :]
+                rounded = []
                 for c in range(rows // DH):
-                    lanes = weights[:, c * DH : (c + 1) * DH]
+                    lanes = jnp.exp2((scores[d][:, c * DH : (c + 1) * DH] - offset) * factor)
                     total = lanes if total is None else total + lanes
+                    rounded.append(lanes.astype(jnp.bfloat16))
                 product = jnp.dot(
-                    weights.astype(jnp.bfloat16),
+                    jnp.concatenate(rounded, axis=1),
                     vbuf[g, place, :],
                     preferred_element_type=jnp.float32,
                 )
@@ -313,7 +340,9 @@
     @pl.loop(0, HK)
     def _(g):
         for_direct(lambda d: end_send(direct, g, d))
-        for_relay(lambda d: end_send(relay, g, d))
+        for_forward(lambda d: end_send(forward, g, d))
+        for_relay(lambda d: end_send(relay, g, d), False)
+        for_relay(lambda d: end_send(relay, g, d), True)
 
     @pl.loop(sent_steps, steps)
     def _(step):

time: 57.9 us -> 57.5 us (level)
  no operation moved by 1% of the time
where the time goes in v3:
time: 57.5 us; the launch traced here: 57.4 us
  Pallas kernels  56.1 us (98%)
  local copies, waits for them, and re-layouts  1.32 us (2%)
    pallas_call x1, Pallas kernels, shards(): pl.pallas_call(functools.partial(kernel, n_pipe, n_ctx, window, rows), ou...  56.1 us
    unnamed x1, local copies, waits for them, and re-layouts  1.32 us

profile of v3, /device:TPU:0, one launch (start us, length us, event | category | flops | bytes accessed | tf_op | source)
XLA Modules:
  0.0 57.4 jit_solution(3369904594774126174)
XLA Ops:
  0.0 56.1 %relay_attention.1 = bf16[256,4096]{1,0:T(8,128)(2,1)S(1)} custom-call(s32[1,8]{1,0:T(1,128)} %doc_hbm.1, bf16[256,4096]{1,0:T(8,128)(2,1)} %bitcast.5, bf16[256,512]{1,0:T(8,128)(2,1)} %bitcast.6, bf16[256,512]{1,0:T(8,128)(2,1)} %bitcast.7), custom_call_target="tpu_custom_call" | custom-call | tf_op jit(solution)/shard_map/relay_attention/pallas_call | solution.py:364
  56.1 1.3 %copy.6 = bf16[1,256,4096]{2,1,0:T(8,128)(2,1)} copy(bf16[1,256,4096]{2,1,0:T(8,128)(2,1)S(1)} %bitcast.4) | data formatting | bytes 4194304

commit v4 on v3

--- a/solution.py
+++ b/solution.py
@@ -55,20 +55,25 @@
     sent_steps = moved * group_steps
     last = window - 1
 
+    core = lax.rem(ctx, 2)
+    odd_chip = lax.rem(ctx // 2, 2) == 1
+    even_chip = lax.rem(ctx // 2, 2) == 0
+    turn = 1 - 2 * core
+    sibling = ctx + turn
     barrier = pltpu.get_barrier_semaphore()
-    pl.semaphore_signal(barrier, inc=1, device_id=(left, ctx), device_id_type=MESH)
-    pl.semaphore_signal(barrier, inc=1, device_id=(right, ctx), device_id_type=MESH)
-    sibling_core = ctx + 1 - 2 * lax.rem(ctx, 2)
-    pl.semaphore_signal(barrier, inc=1, device_id=(pipe, sibling_core), device_id_type=MESH)
-    for d in range(2, window, 2):
-
-        @pl.when(ctx >= d)
-        def _():
-            pl.semaphore_signal(barrier, inc=1, device_id=(pipe, ctx - d), device_id_type=MESH)
-
-        @pl.when(ctx + d < n_ctx)
-        def _():
-            pl.semaphore_signal(barrier, inc=1, device_id=(pipe, ctx + d), device_id_type=MESH)
+
+    def greet(pipe_to, ctx_to):
+        pl.semaphore_signal(barrier, inc=1, device_id=(pipe_to, ctx_to), device_id_type=MESH)
+
+    greet(left, ctx)
+    pl.when((core == 1) | (ctx >= 2))(lambda: greet(pipe, sibling))
+    pl.when(odd_chip)(lambda: greet(pipe, lax.rem(ctx + n_ctx - 2, n_ctx)))
+    pl.when(even_chip & (ctx >= 2))(lambda: greet(pipe, lax.rem(ctx + 2, n_ctx)))
+    met = 1 + jnp.where((core == 0) | (ctx >= 2), 1, 0)
+    met = met + jnp.where(even_chip, 1, 0) + jnp.where(odd_chip & (ctx >= 4), 1, 0)
+    for d in range(4, window, 2):
+        pl.when(ctx >= d)(lambda d=d: greet(pipe, lax.rem(ctx + n_ctx - d, n_ctx)))
+        met = met + jnp.where(ctx + d < n_ctx, 1, 0)
 
     def own_copies(g):
         cols = pl.ds(pl.multiple_of(g * DH, DH), DH)
@@ -100,15 +105,8 @@
     def direct(g, d):
         return kv_copies(g, 0, d, lax.rem(ctx + d, n_ctx))
 
-    core = lax.rem(ctx, 2)
-    turn = 1 - 2 * core
-    sibling = ctx + turn
-
     def relay(g, d):
         return kv_copies(g, d, d + turn, sibling)
-
-    odd_chip = lax.rem(ctx // 2, 2) == 1
-    even_chip = lax.rem(ctx // 2, 2) == 0
 
     def forward(g, d):
         return kv_copies(g, d, d - 2, lax.rem(ctx + n_ctx - 2, n_ctx))
@@ -190,6 +188,10 @@
             copy.start()
         q_copy(g).start()
 
+    pl.semaphore_wait(barrier, met)
+    for at in (0, 1, 3):
+        moved_copies()[at].start()
+
     doc_copy.wait()
     bias[0] = jnp.zeros(bias.shape[1:], jnp.float32)
     own_doc = doc_ref[0, ctx]
@@ -198,22 +200,7 @@
         seen = (doc_ref[0, block] == own_doc) & (ctx >= d)
         bias[0, d : d + 1, :] = jnp.full((1, DH), jnp.where(seen, 0.0, HIDDEN), jnp.float32)
 
-    for d in range(1, window):
-
-        @pl.when(ctx < d)
-        def _():
-            place = pl.ds((last - d) * rows, rows)
-            for g in range(HK):
-                kbuf[g, place, :] = jnp.zeros((rows, DH), kbuf.dtype)
-                vbuf[g, place, :] = jnp.zeros((rows, DH), vbuf.dtype)
-
-    met = 3
-    for d in range(2, window, 2):
-        met = met + jnp.where(ctx >= d, 1, 0) + jnp.where(ctx + d < n_ctx, 1, 0)
-    pl.semaphore_wait(barrier, met)
-
-    for copy in moved_copies():
-        copy.start()
+    moved_copies()[2].start()
 
     def start_direct(g):
         if g < moved:
@@ -240,6 +227,15 @@
             pl.when(ctx >= d)(functools.partial(wait_block, g, d))
 
     start_direct(0)
+    for d in range(1, window):
+
+        @pl.when(ctx < d)
+        def _():
+            place = pl.ds((last - d) * rows, rows)
+            for g in range(HK):
+                kbuf[g, place, :] = jnp.zeros((rows, DH), kbuf.dtype)
+                vbuf[g, place, :] = jnp.zeros((rows, DH), vbuf.dtype)
+
     pass_on(0)
     start_direct(1)
     pass_late(0)

time: 57.5 us -> 57.5 us (level)
  no operation moved by 1% of the time
where the time goes in v4:
time: 57.5 us; the launch traced here: 57.4 us
  Pallas kernels  56.1 us (98%)
  local copies, waits for them, and re-layouts  1.32 us (2%)
    pallas_call x1, Pallas kernels, shards(): pl.pallas_call(functools.partial(kernel, n_pipe, n_ctx, window, rows), ou...  56.1 us
    unnamed x1, local copies, waits for them, and re-layouts  1.32 us

profile of v4, /device:TPU:0, one launch (start us, length us, event | category | flops | bytes accessed | tf_op | source)
XLA Modules:
  0.0 57.4 jit_solution(10655323045512010656)
XLA Ops:
  0.0 56.1 %relay_attention.1 = bf16[256,4096]{1,0:T(8,128)(2,1)S(1)} custom-call(s32[1,8]{1,0:T(1,128)} %doc_hbm.1, bf16[256,4096]{1,0:T(8,128)(2,1)} %bitcast.5, bf16[256,512]{1,0:T(8,128)(2,1)} %bitcast.6, bf16[256,512]{1,0:T(8,128)(2,1)} %bitcast.7), custom_call_target="tpu_custom_call" | custom-call | tf_op jit(solution)/shard_map/relay_attention/pallas_call | solution.py:360
  56.1 1.3 %copy.6 = bf16[1,256,4096]{2,1,0:T(8,128)(2,1)} copy(bf16[1,256,4096]{2,1,0:T(8,128)(2,1)S(1)} %bitcast.4) | data formatting | bytes 4194304

commit v5 on v4

--- a/solution.py
+++ b/solution.py
@@ -12,7 +12,7 @@
 HK = 4
 DH = 128
 PER_GROUP = HQ // HK
-STEP_HEADS = 2
+STEP_HEADS = 1
 HIDDEN = 1e30
 MESH = pl.DeviceIdType.MESH
 

time: 57.5 us -> 58 us (level)
  no operation moved by 1% of the time
where the time goes in v5:
time: 58 us; the launch traced here: 57.8 us
  Pallas kernels  56.5 us (97%)
  local copies, waits for them, and re-layouts  1.32 us (2%)
    pallas_call x1, Pallas kernels, shards(): pl.pallas_call(functools.partial(kernel, n_pipe, n_ctx, window, rows), ou...  56.5 us
    unnamed x1, local copies, waits for them, and re-layouts  1.32 us

profile of v5, /device:TPU:0, one launch (start us, length us, event | category | flops | bytes accessed | tf_op | source)
XLA Modules:
  0.0 57.8 jit_solution(17696318568470233100)
XLA Ops:
  0.0 56.5 %relay_attention.1 = bf16[256,4096]{1,0:T(8,128)(2,1)S(1)} custom-call(s32[1,8]{1,0:T(1,128)} %doc_hbm.1, bf16[256,4096]{1,0:T(8,128)(2,1)} %bitcast.5, bf16[256,512]{1,0:T(8,128)(2,1)} %bitcast.6, bf16[256,512]{1,0:T(8,128)(2,1)} %bitcast.7), custom_call_target="tpu_custom_call" | custom-call | tf_op jit(solution)/shard_map/relay_attention/pallas_call | solution.py:360
  56.5 1.3 %copy.6 = bf16[1,256,4096]{2,1,0:T(8,128)(2,1)} copy(bf16[1,256,4096]{2,1,0:T(8,128)(2,1)S(1)} %bitcast.4) | data formatting | bytes 4194304
